TPU v7x, 32 devices: a whole 2x2x4 slice. The times are simulated.
32 devices in a mesh: ctx: 8 (over z, y), ch: 4 (over x, core).
Axes of the slice: x: 2, y: 2, z: 4, core: 2. Of those that a mesh axis runs over, the one named last changes fastest.
Arguments:
- queries: bfloat16 [2048, 4096], P('ctx', 'ch'), may hold values from -6 to 6
- keys: bfloat16 [2048, 4096], P('ctx', 'ch'), may hold values from -6 to 6
- values: bfloat16 [2048, 4096], P('ctx', 'ch'), may hold values from -6 to 6
- long_filter: float32 [2048, 4096], P('ctx', 'ch'), may hold values from -1.05 to 1.05
- short_filters: float32 [3, 3, 4096], P(None, None, 'ch'), may hold values from -3.6 to 3.6
- skip: float32 [4096], P('ch'), may hold values from -1 to 1
- w_out: bfloat16 [4096, 8192], P('ch'), may hold values from -0.09375 to 0.09375
- d_out: bfloat16 [2048, 8192], P('ctx', 'ch'), may hold values from -6 to 6
Outputs:
- d_queries: bfloat16 [2048, 4096], P('ctx', 'ch')
- d_keys: bfloat16 [2048, 4096], P('ctx', 'ch')
- d_values: bfloat16 [2048, 4096], P('ctx', 'ch')
- d_long: float32 [2048, 4096], P('ctx', 'ch')
- d_short: float32 [3, 3, 4096], P(None, None, 'ch')
- d_skip: float32 [4096], P('ch')
All inputs are finite; a program needn't handle non-finite values.
Results may differ from a plain program's by a relative error of at most 0.0049.
Values may be sent and summed in bfloat16 or wider, within the bound.
A program may use at most 128 MiB of HBM per device.

v0:
```python
import math
import jax
import jax.numpy as jnp
from jax import lax
from jax.sharding import PartitionSpec as P


def passed_along(block, axis, distance):
    devices = range(lax.axis_size(axis))
    route = [(i - distance, i) for i in devices if i - distance in devices]
    return lax.ppermute(block, axis, route)


def phases(left_index, right_index, modulus):
    product = left_index[:, None] * right_index[None, :] % modulus
    angle = product.astype(jnp.float32) * (2.0 * math.pi / modulus)
    return (jnp.cos(angle), jnp.sin(angle))


def mat_apply(table, data, form):
    return jnp.einsum(form, table, data, precision=lax.Precision.HIGHEST)


def fine_forward(fine_cos, fine_sin, real_part, imag_part):
    spec_real = mat_apply(fine_cos, real_part, "kb,sbc->skc") + mat_apply(
        fine_sin, imag_part, "kb,sbc->skc"
    )
    spec_imag = mat_apply(fine_cos, imag_part, "kb,sbc->skc") - mat_apply(
        fine_sin, real_part, "kb,sbc->skc"
    )
    return (spec_real, spec_imag)


def fine_inverse(fine_cos, fine_sin, real_part, imag_part):
    back_real = mat_apply(fine_cos, real_part, "bk,skc->sbc") - mat_apply(
        fine_sin, imag_part, "bk,skc->sbc"
    )
    back_imag = mat_apply(fine_cos, imag_part, "bk,skc->sbc") + mat_apply(
        fine_sin, real_part, "bk,skc->sbc"
    )
    return (back_real, back_imag)


def forward_half(regrouped, ctx_size, position, block_len, total_len):
    seq_rows = ctx_size * block_len
    coarse = jnp.arange(ctx_size, dtype=jnp.int32)
    coarse_cos, coarse_sin = phases(coarse, coarse, 2 * ctx_size)
    signs = 1.0 - 2.0 * (coarse % 2).astype(jnp.float32)
    first_row = (coarse == 0)[:, None]
    coef_real = jnp.where(first_row, jnp.float32(1.0), coarse_cos)
    coef_imag = jnp.where(first_row, signs[None, :], -coarse_sin)
    first_real = mat_apply(coef_real, regrouped, "ka,sabc->skbc")
    first_imag = mat_apply(coef_imag, regrouped, "ka,sabc->skbc")
    fine_global = position * block_len + jnp.arange(block_len, dtype=jnp.int32)
    twist_cos, twist_sin = phases(coarse, fine_global, total_len)
    twist_cos = twist_cos[None, :, :, None]
    twist_sin = twist_sin[None, :, :, None]
    second_real = first_real * twist_cos + first_imag * twist_sin
    second_imag = first_imag * twist_cos - first_real * twist_sin
    moved = lax.all_to_all(
        jnp.stack([second_real, second_imag], axis=1),
        "ctx",
        split_axis=2,
        concat_axis=3,
        tiled=True,
    )
    packed_real = moved[:, 0, 0]
    packed_imag = moved[:, 1, 0]
    fine_index = jnp.arange(seq_rows, dtype=jnp.int32)
    fine_cos, fine_sin = phases(fine_index, fine_index, seq_rows)
    shift_cos, shift_sin = phases(fine_index, jnp.ones((1,), jnp.int32), 2 * seq_rows)
    shift_cos = shift_cos[None]
    shift_sin = shift_sin[None]

    def corner_slots(operands):
        low_part, top_part = operands
        main_real, main_imag = fine_forward(fine_cos, fine_sin, low_part, jnp.zeros_like(low_part))
        top_real, top_imag = fine_forward(
            fine_cos, fine_sin, top_part * shift_cos, -top_part * shift_sin
        )
        return (jnp.stack([main_real, top_real], axis=1), jnp.stack([main_imag, top_imag], axis=1))

    def plain_slots(operands):
        real_part, imag_part = operands
        main_real, main_imag = fine_forward(fine_cos, fine_sin, real_part, imag_part)
        empty = jnp.zeros_like(main_real)
        return (jnp.stack([main_real, empty], axis=1), jnp.stack([main_imag, empty], axis=1))

    return lax.cond(position == 0, corner_slots, plain_slots, (packed_real, packed_imag))


def inverse_half(spec_real, spec_imag, ctx_size, position, block_len, total_len):
    seq_rows = spec_real.shape[2]
    fine_index = jnp.arange(seq_rows, dtype=jnp.int32)
    fine_cos, fine_sin = phases(fine_index, fine_index, seq_rows)
    shift_cos, shift_sin = phases(fine_index, jnp.ones((1,), jnp.int32), 2 * seq_rows)
    shift_cos = shift_cos[None]
    shift_sin = shift_sin[None]

    def corner_back(operands):
        slot_real, slot_imag = operands
        low_real, low_imag = fine_inverse(fine_cos, fine_sin, slot_real[:, 0], slot_imag[:, 0])
        top_real, top_imag = fine_inverse(fine_cos, fine_sin, slot_real[:, 1], slot_imag[:, 1])
        return (low_real, top_real * shift_cos - top_imag * shift_sin)

    def plain_back(operands):
        slot_real, slot_imag = operands
        return fine_inverse(fine_cos, fine_sin, slot_real[:, 0], slot_imag[:, 0])

    back_real, back_imag = lax.cond(position == 0, corner_back, plain_back, (spec_real, spec_imag))
    sending = jnp.stack([back_real, back_imag], axis=1)[:, :, None]
    returned = lax.all_to_all(sending, "ctx", split_axis=3, concat_axis=2, tiled=True)
    part_real = returned[:, 0]
    part_imag = returned[:, 1]
    coarse = jnp.arange(ctx_size, dtype=jnp.int32)
    fine_global = position * block_len + jnp.arange(block_len, dtype=jnp.int32)
    twist_cos, twist_sin = phases(coarse, fine_global, total_len)
    twist_cos = twist_cos[None, :, :, None]
    twist_sin = twist_sin[None, :, :, None]
    turned_real = part_real * twist_cos - part_imag * twist_sin
    turned_imag = part_imag * twist_cos + part_real * twist_sin
    coarse_cos, coarse_sin = phases(coarse, coarse, 2 * ctx_size)
    signs = 1.0 - 2.0 * (coarse % 2).astype(jnp.float32)
    first_col = (coarse == 0)[None, :]
    coef_real = jnp.where(first_col, jnp.float32(1.0), 2.0 * coarse_cos)
    coef_imag = jnp.where(first_col, signs[:, None], -2.0 * coarse_sin)
    result = mat_apply(coef_real, turned_real, "ak,skbc->sabc") + mat_apply(
        coef_imag, turned_imag, "ak,skbc->sabc"
    )
    return result / total_len


def per_device(queries, keys, values, long_filter, short_filters, skip, w_out, d_out):
    ctx_size = lax.axis_size("ctx")
    position = lax.axis_index("ctx")
    seq_rows = queries.shape[0]
    width = queries.shape[1]
    block_len = seq_rows // ctx_size
    total_len = 2 * ctx_size * seq_rows
    tap_count = short_filters.shape[1]
    rim_width = tap_count - 1
    streams = jnp.stack([queries, keys, values])
    before = passed_along(streams[:, seq_rows - rim_width :, :], "ctx", 1)
    extended = jnp.concatenate([before, streams], axis=1).astype(jnp.float32)
    filtered = jnp.zeros((3, seq_rows, width), jnp.float32)
    for j in range(tap_count):
        filtered = (
            filtered
            + short_filters[:, j, None, :]
            * extended[:, rim_width - j : rim_width - j + seq_rows, :]
        )
    mixed = filtered[1] * filtered[2]
    accumulated = lax.dot_general(
        lax.all_gather(d_out, "ch", axis=1, tiled=True),
        w_out,
        (((1,), (1,)), ((), ())),
        preferred_element_type=jnp.float32,
    )
    grad_o = lax.optimization_barrier(accumulated.astype(jnp.bfloat16)).astype(jnp.float32)
    grad_y = grad_o * filtered[0]
    signals = jnp.stack([mixed, long_filter, grad_y])
    regrouped = lax.all_to_all(signals[:, None], "ctx", split_axis=2, concat_axis=1, tiled=True)
    spec_real, spec_imag = forward_half(regrouped, ctx_size, position, block_len, total_len)
    mix_re, mix_im = (spec_real[0], spec_imag[0])
    fil_re, fil_im = (spec_real[1], spec_imag[1])
    grad_re, grad_im = (spec_real[2], spec_imag[2])
    out_re = mix_re * fil_re - mix_im * fil_im
    out_im = mix_re * fil_im + mix_im * fil_re
    back_re = grad_re * fil_re + grad_im * fil_im
    back_im = grad_im * fil_re - grad_re * fil_im
    corr_re = grad_re * mix_re + grad_im * mix_im
    corr_im = grad_im * mix_re - grad_re * mix_im
    fields = inverse_half(
        jnp.stack([out_re, back_re, corr_re]),
        jnp.stack([out_im, back_im, corr_im]),
        ctx_size,
        position,
        block_len,
        total_len,
    )
    timed = lax.all_to_all(fields, "ctx", split_axis=1, concat_axis=2, tiled=True).reshape(
        3, seq_rows, width
    )
    conv_y = timed[0]
    conv_back = timed[1]
    d_long = timed[2]
    y_full = conv_y + skip[None, :] * mixed
    grad_mixed = conv_back + skip[None, :] * grad_y
    grads = jnp.stack([grad_o * y_full, grad_mixed * filtered[2], grad_mixed * filtered[1]])
    after = passed_along(grads[:, :rim_width, :], "ctx", -1)
    grads_ext = jnp.concatenate([grads, after], axis=1)
    stream_grads = jnp.zeros((3, seq_rows, width), jnp.float32)
    tap_terms = []
    for j in range(tap_count):
        stream_grads = (
            stream_grads + short_filters[:, j, None, :] * grads_ext[:, j : j + seq_rows, :]
        )
        tap_terms.append(
            jnp.sum(grads * extended[:, rim_width - j : rim_width - j + seq_rows, :], axis=1)
        )
    short_terms = jnp.stack(tap_terms, axis=1)
    skip_term = jnp.sum(grad_y * mixed, axis=0)
    d_short, d_skip = lax.psum((short_terms, skip_term), "ctx")
    return (
        stream_grads[0].astype(jnp.bfloat16),
        stream_grads[1].astype(jnp.bfloat16),
        stream_grads[2].astype(jnp.bfloat16),
        d_long,
        d_short,
        d_skip,
    )


def solution(mesh):
    in_specs = (
        P("ctx", "ch"),
        P("ctx", "ch"),
        P("ctx", "ch"),
        P("ctx", "ch"),
        P(None, None, "ch"),
        P("ch"),
        P("ch", None),
        P("ctx", "ch"),
    )
    out_specs = (
        P("ctx", "ch"),
        P("ctx", "ch"),
        P("ctx", "ch"),
        P("ctx", "ch"),
        P(None, None, "ch"),
        P("ch"),
    )
    return jax.shard_map(
        per_device, mesh=mesh, in_specs=in_specs, out_specs=out_specs, check_vma=False
    )
```

profile of v0, /device:TPU:0, one launch (start us, length us, event | category | flops | bytes accessed | tf_op | source)
XLA Modules:
  0.0 732.7 jit_solution(4294775864192392248)
XLA Ops:
  8.7 4.9 collective-permute-start
  18.4 28.4 %all-gather.2.cloned.1.call-done = bf16[256,8192]{1,0:T(8,128)(2,1)} async-done(((bf16[256,2048]{1,0:T(8,128)(2,1)}), bf16[256,8192]{1,0:T(8,128)(2,1)}) %all-gather.2.cloned.1.call-update) | async-done | bytes 4194320 | tf_op jit(solution)/shard_map/all_gather | solution.py:154
  46.8 12.4 %convolution_convert_fusion = bf16[256,1024]{1,0:T(8,128)(2,1)} fusion(bf16[256,8192]{1,0:T(8,128)(2,1)} %all-gather.2.cloned.1.call-done, bf16[1024,8192]{1,0:T(8,128)(2,1)} %param.18), kind=kOutput, calls=%fused_computation.137 | convolution fusion | flops 4295229440 | bytes 21495808 | tf_op jit(solution)/shard_map/dot_general | solution.py:153
  61.3 4.9 copy.66
  66.1 5.7 all-to-all-start
  72.0 70.8 %all-to-all-done = f32[3,1,256,1024]{3,1,0,2:T(1,128)S(1)} async-done(((f32[3,1,256,1024]{3,1,0,2:T(1,128)}), f32[3,1,256,1024]{3,1,0,2:T(1,128)S(1)}, u32[]{:S(2)}, u32[]{:S(2)}) %all-to-all-start) | async-done | bytes 3145760 | tf_op jit(solution)/shard_map/all_to_all | solution.py:162
  143.5 5.6 fusion.93
  149.1 6.2 fusion.82
  156.6 6.3 copy.70
  168.9 136.6 %all-to-all-done.1 = f32[3,2,8,32,1024]{4,3,0,1,2:T(8,128)} async-done(((f32[3,2,8,32,1024]{4,3,0,1,2:T(8,128)}), f32[3,2,8,32,1024]{4,3,0,1,2:T(8,128)}, u32[]{:S(2)}, u32[]{:S(2)}) %all-to-all-start.1) | async-done | bytes 6291488 | tf_op jit(solution)/shard_map/all_to_all | solution.py:60
  309.9 48.2 %conditional.2 = ((f32[3,2,256,1024]{2,3,0,1:T(8,128)}, f32[3,2,256,1024]{2,3,0,1:T(8,128)})) conditional(s32[]{:T(128)} %convert_element_type.132, (f32[3,256,1024]{2,1,0:T(8,128)S(1)}, f32[256,256]{1,0:T(8,128)S(1)}, f32[3,256,1024]{2,1,0:T(8,128)S(1)}, f32[256,256]{1,0:T(8,128)S(1)}, f32[256,256]{1,0:T(8,128)S(1)}, ...), branch_computations={%region_0.1_spmd.clone, %region_1.2_spmd.clone} | conditional | flops 19338362880 | bytes 130027672 | solution.py:89
  335.6 5.7 fusion.74
  346.6 5.8 subtract_bitcast_fusion.5
  352.4 5.4 pad_maximum_fusion
  358.2 7.8 %multiply_subtract_fusion = (f32[1,2,256,1024]{2,3,0,1:T(8,128)}, f32[1,2,256,1024]{2,3,0,1:T(8,128)}) fusion(f32[3,2,256,1024]{2,3,0,1:T(8,128)} %get-tuple-element.306, f32[3,2,256,1024]{2,3,0,1:T(8,128)} %get-tuple-element.307), kind=kLoop, calls=%fused_computation.124 | loop fusion | flops 3145728 | bytes 16777216 | tf_op jit(solution)/shard_map/sub | solution.py:172
  377.7 56.3 %conditional.3 = (f32[3,1,256,1024]{3,1,0,2:T(1,128)}, f32[3,1,256,1024]{3,1,0,2:T(1,128)}) conditional(s32[]{:T(128)} %convert_element_type.132, (f32[3,2,256,1024]{2,3,0,1:T(8,128)S(1)}, f32[256,256]{1,0:T(8,128)S(1)}, f32[3,2,256,1024]{2,3,0,1:T(8,128)S(1)}, f32[256,256]{1,0:T(8,128)S(1)}, f32[256,256]{1,0:T(8,128)S(1)}, ...), branch_computations={%region_2.3_spmd, %region_3.4_spmd} | conditional | flops 14500233216 | bytes 165152912 | solution.py:110
  405.7 8.6 %copy.92 = f32[3,1,256,1024]{3,1,0,2:T(1,128)} copy(f32[3,1,256,1024]{2,3,0,1:T(8,128)} %subtract_bitcast_fusion.2) | data formatting | bytes 6291456 | tf_op jit(solution)/shard_map/cond | solution.py:110
  428.0 5.6 copy.94
  433.9 8.5 %maximum_bitcast_fusion = f32[3,2,1,256,1024]{4,1,0,2,3:T(2,128)S(1)} fusion(f32[3,1,256,1024]{3,1,0,2:T(1,128)} %get-tuple-element.309, f32[3,1,256,1024]{3,1,0,2:T(1,128)} %get-tuple-element.308), kind=kLoop, calls=%fused_computation.86 | loop fusion | flops 1572864 | bytes 12582912 | tf_op jit(solution)/shard_map/broadcast_in_dim | solution.py:111
  442.4 139.4 %all_to_all.45 = f32[3,2,1,256,1024]{4,1,0,2,3:T(2,128)S(1)} all-to-all(f32[3,2,1,256,1024]{4,1,0,2,3:T(2,128)S(1)} %maximum_bitcast_fusion), channel_id=1, replica_groups=mesh['ctx'=8,'ch'=4] {'ctx'}, dimensions={3} | all-to-all | bytes 12582912 | tf_op jit(solution)/shard_map/all_to_all | solution.py:112
  585.0 7.4 %fusion.85 = f32[3,32,1024,8]{2,3,1,0:T(8,128)S(1)} fusion(f32[3,1,8,32,1024]{4,3,2,1,0:T(8,128)S(1)} %get-tuple-element.326, f32[3,1,8,32,1024]{4,3,2,1,0:T(8,128)S(1)} %get-tuple-element.325, f32[8,32]{0,1:T(8,128)S(1)} %get-tuple-element.344, f32[8,32]{0,1:T(8,128)S(1)} %get-tuple-element.343, f32[8]{0:T(128)S(1)} %fusion.159, ...), kind=kOutput, calls=%fused_computation.111 | convolution fusion | flops 77857792 | bytes 9439272 | tf_op jit(solution)/shard_map/ak,skbc->sabc/dot_general | solution.py:21
  592.4 7.9 %multiply_bitcast_fusion = f32[3,8,32,1024]{3,1,2,0:T(8,128)S(1)} fusion(f32[3,32,1024,8]{2,3,1,0:T(8,128)S(1)} %fusion.85, f32[3,1,8,32,1024]{4,3,2,1,0:T(8,128)S(1)} %get-tuple-element.326, f32[3,1,8,32,1024]{4,3,2,1,0:T(8,128)S(1)} %get-tuple-element.325, f32[8,32]{0,1:T(8,128)S(1)} %get-tuple-element.344, f32[8,32]{0,1:T(8,128)S(1)} %get-tuple-element.343, ...), kind=kOutput, calls=%fused_computation.110 | convolution fusion | flops 79430656 | bytes 12584968 | tf_op jit(solution)/shard_map/ak,skbc->sabc/dot_general | solution.py:21
  602.1 73.8 %all_to_all.46 = f32[3,8,32,1024]{3,2,0,1:T(8,128)S(1)} all-to-all(f32[3,8,32,1024]{3,2,0,1:T(8,128)S(1)} %copy.81), channel_id=1, replica_groups=mesh['ctx'=8,'ch'=4] {'ctx'}, dimensions={1} | all-to-all | bytes 6291456 | tf_op jit(solution)/shard_map/all_to_all | solution.py:181
  688.1 35.7 %all-reduce.2 = (f32[3,3,1024]{2,0,1:T(4,128)S(1)}, f32[1024]{0:T(1024)}) all-reduce(f32[3,3,1024]{2,0,1:T(4,128)S(1)} %pad_maximum_fusion.7, f32[1024]{0:T(1024)S(1)} %get-tuple-element.332), channel_id=1, replica_groups=mesh['ctx'=8,'ch'=4] {'ctx'}, use_global_device_ids=true, to_apply=%region_7.8 | all-reduce | flops 10240 | bytes 81920 | tf_op jit(solution)/shard_map/psum | solution.py:203
  (119 shorter events, 95.7 us)
Async XLA Ops:
  7.2 7.8 %copy-start.23 = (bf16[256,1024]{1,0:T(8,128)(2,1)S(1)}, bf16[256,1024]{1,0:T(8,128)(2,1)}, u32[]{:S(2)}) copy-start(bf16[256,1024]{1,0:T(8,128)(2,1)} %param.14) | copy-start | bytes 1572868
  7.2 7.8 %copy-start.24 = (bf16[256,1024]{1,0:T(8,128)(2,1)S(1)}, bf16[256,1024]{1,0:T(8,128)(2,1)}, u32[]{:S(2)}) copy-start(bf16[256,1024]{1,0:T(8,128)(2,1)} %param.13) | copy-start | bytes 1572868
  7.2 7.8 %copy-start.25 = (bf16[256,1024]{1,0:T(8,128)(2,1)S(1)}, bf16[256,1024]{1,0:T(8,128)(2,1)}, u32[]{:S(2)}) copy-start(bf16[256,1024]{1,0:T(8,128)(2,1)} %param.12) | copy-start | bytes 1572868
  7.2 39.6 %all-gather.2.cloned.1.call-start = ((), (), s32[]{:S(2)}) async-start(), calls=%async_computation.4 | async-start | bytes 5242880 | tf_op jit(solution)/shard_map/all_gather | solution.py:154
  8.7 6.3 collective-permute-start
  17.1 42.0 %copy-start.15 = (f32[3,256,1024]{2,1,0:T(8,128)}, f32[3,256,1024]{2,1,0:T(8,128)S(1)}, u32[]{:S(2)}) copy-start(f32[3,256,1024]{2,1,0:T(8,128)S(1)} %multiply_add_fusion) | copy-start | bytes 9437188
  66.1 76.6 %all-to-all-start = ((f32[3,1,256,1024]{3,1,0,2:T(1,128)}), f32[3,1,256,1024]{3,1,0,2:T(1,128)S(1)}, u32[]{:S(2)}, u32[]{:S(2)}) async-start(f32[3,1,256,1024]{3,1,0,2:T(1,128)} %copy.66), calls=%async_computation | async-start | bytes 6291456 | tf_op jit(solution)/shard_map/all_to_all | solution.py:162
  163.0 142.5 %all-to-all-start.1 = ((f32[3,2,8,32,1024]{4,3,0,1,2:T(8,128)}), f32[3,2,8,32,1024]{4,3,0,1,2:T(8,128)}, u32[]{:S(2)}, u32[]{:S(2)}) async-start(f32[3,2,8,32,1024]{4,3,0,1,2:T(8,128)} %copy.70), calls=%async_computation.1 | async-start | bytes 12582912 | tf_op jit(solution)/shard_map/all_to_all | solution.py:60
  168.8 141.1 %copy-start.11 = (f32[256,256]{1,0:T(8,128)}, f32[256,256]{1,0:T(8,128)S(1)}, u32[]{:S(2)}) copy-start(f32[256,256]{1,0:T(8,128)S(1)} %get-tuple-element.347) | copy-start | bytes 786436
  332.7 2.9 copy-start.3
  358.2 7.9 %copy-start.8 = (f32[3,2,256,1024]{2,3,0,1:T(8,128)S(1)}, f32[3,2,256,1024]{2,3,0,1:T(8,128)}, u32[]{:S(2)}) copy-start(f32[3,2,256,1024]{2,3,0,1:T(8,128)} %get-tuple-element.307) | copy-start | bytes 18874372
  358.2 9.8 %copy-start.9 = (f32[3,2,256,1024]{2,3,0,1:T(8,128)S(1)}, f32[3,2,256,1024]{2,3,0,1:T(8,128)}, u32[]{:S(2)}) copy-start(f32[3,2,256,1024]{2,3,0,1:T(8,128)} %get-tuple-element.306) | copy-start | bytes 18874372
  372.0 3.8 copy-start.18
  372.0 4.1 copy-start.19
  372.0 4.7 copy-start.20
  396.7 2.9 copy-start.4
  396.7 4.6 copy-start.6
  414.3 4.8 copy-start.5
  419.1 2.8 copy-start.7
  679.5 6.5 copy-start.1
  679.5 6.5 copy-start.28
  679.5 6.5 copy-start.30
  679.5 6.5 copy-start.32
  679.5 6.0 collective-permute-start.1
  (14 other events, 28.0 us)
Sparse Core Ops, SparseCore 0:
  9.6 37.1 all-gather.1
where the time goes:
time: 741 us; the launch traced here: 733 us
  blocking collectives  249 us (34%)
  waiting for transfers between devices  241 us (33%)
  matrix products  88.5 us (12%)
  local copies, waits for them, and re-layouts  51.7 us (7%)
  other arithmetic  41.7 us (6%)
  loops' own time  29 us (4%)
  starting transfers between devices  16.9 us (2%)
  between operations  14.7 us (2%)
    all_to_all x1, blocking collectives, inverse_half(): lax.all_to_all(sending, 'ctx', split_axis=3, concat_axis=2, tiled=True)  139 us
    all_to_all x1, waiting for transfers between devices, forward_half(): lax.all_to_all(jnp.stack([second_real, second_imag], axis=1), 'ctx', spli...  137 us
    dot_general x18, matrix products, mat_apply(): return jnp.einsum(form, table, data, precision=lax.Precision.HIGHEST)  76.1 us
    all_to_all x1, blocking collectives, per_device(): lax.all_to_all(fields, 'ctx', split_axis=1, concat_axis=2, tiled=True)  73.8 us
    all_to_all x1, waiting for transfers between devices, per_device(): lax.all_to_all(signals[:, None], 'ctx', split_axis=2, concat_axis=1, tile...  70.8 us
    psum x1, blocking collectives, per_device(): d_short, d_skip = lax.psum((short_terms, skip_term), 'ctx')  35.7 us
    all_gather x1, waiting for transfers between devices, per_device(): lax.all_gather(d_out, 'ch', axis=1, tiled=True)  28.4 us
    another operation x1, loops' own time, inverse_half(): lax.cond(position == 0, corner_back, plain_back, (spec_real, spec_imag))  19.5 us
  transfers between devices with their start and end apart: 5, of which 5 were waited for; matrix products, arithmetic and copies ran while one was open for 1% of the time, Pallas kernels for 0%

commit v1 on v0

--- a/solution.py
+++ b/solution.py
@@ -109,7 +109,10 @@
 
     back_real, back_imag = lax.cond(position == 0, corner_back, plain_back, (spec_real, spec_imag))
     sending = jnp.stack([back_real, back_imag], axis=1)[:, :, None]
-    returned = lax.all_to_all(sending, "ctx", split_axis=3, concat_axis=2, tiled=True)
+    returned = jnp.concatenate(
+        lax.all_to_all(jnp.stack(jnp.split(sending, lax.axis_size("ctx"), axis=3)), "ctx", 0, 0),
+        axis=2,
+    )
     part_real = returned[:, 0]
     part_imag = returned[:, 1]
     coarse = jnp.arange(ctx_size, dtype=jnp.int32)

time: 741 us -> 716 us (0.966)
    cond x2, local copies, waits for them, and re-layouts: 14.2 us -> 5.94 us  [inverse_half(): lax.cond(position == 0, corner_back, plain_back, (spec_real, spec_imag))]
where the time goes in v1:
time: 716 us; the launch traced here: 708 us
  blocking collectives  249 us (35%)
  waiting for transfers between devices  241 us (34%)
  matrix products  81.9 us (11%)
  local copies, waits for them, and re-layouts  44.8 us (6%)
  other arithmetic  36.8 us (5%)
  loops' own time  22.2 us (3%)
  starting transfers between devices  17 us (2%)
  between operations  15 us (2%)
    all_to_all x1, blocking collectives, inverse_half(): lax.all_to_all(jnp.stack(jnp.split(sending, lax.axis_size('ctx'), axis=3)...  139 us
    all_to_all x1, waiting for transfers between devices, forward_half(): lax.all_to_all(jnp.stack([second_real, second_imag], axis=1), 'ctx', spli...  137 us
    all_to_all x1, blocking collectives, per_device(): lax.all_to_all(fields, 'ctx', split_axis=1, concat_axis=2, tiled=True)  73.8 us
    all_to_all x1, waiting for transfers between devices, per_device(): lax.all_to_all(signals[:, None], 'ctx', split_axis=2, concat_axis=1, tile...  70.7 us
    dot_general x18, matrix products, mat_apply(): return jnp.einsum(form, table, data, precision=lax.Precision.HIGHEST)  69.6 us
    psum x1, blocking collectives, per_device(): d_short, d_skip = lax.psum((short_terms, skip_term), 'ctx')  35.7 us
    all_gather x1, waiting for transfers between devices, per_device(): lax.all_gather(d_out, 'ch', axis=1, tiled=True)  28.4 us
  transfers between devices with their start and end apart: 5, of which 5 were waited for; matrix products, arithmetic and copies ran while one was open for 1% of the time, Pallas kernels for 0%

profile of v1, /device:TPU:0, one launch (start us, length us, event | category | flops | bytes accessed | tf_op | source)
XLA Modules:
  0.0 707.7 jit_solution(1758166363836495835)
XLA Ops:
  8.7 4.9 collective-permute-start
  18.4 28.4 %all-gather.2.cloned.1.call-done = bf16[256,8192]{1,0:T(8,128)(2,1)} async-done(((bf16[256,2048]{1,0:T(8,128)(2,1)}), bf16[256,8192]{1,0:T(8,128)(2,1)}) %all-gather.2.cloned.1.call-update) | async-done | bytes 4194320 | tf_op jit(solution)/shard_map/all_gather | solution.py:157
  46.8 12.4 %convolution_convert_fusion = bf16[256,1024]{1,0:T(8,128)(2,1)} fusion(bf16[256,8192]{1,0:T(8,128)(2,1)} %all-gather.2.cloned.1.call-done, bf16[1024,8192]{1,0:T(8,128)(2,1)} %param.18), kind=kOutput, calls=%fused_computation.138 | convolution fusion | flops 4295229440 | bytes 21495808 | tf_op jit(solution)/shard_map/dot_general | solution.py:156
  61.3 4.9 copy.76
  66.1 5.7 all-to-all-start
  72.0 70.7 %all-to-all-done = f32[3,1,256,1024]{3,1,0,2:T(1,128)S(1)} async-done(((f32[3,1,256,1024]{3,1,0,2:T(1,128)}), f32[3,1,256,1024]{3,1,0,2:T(1,128)S(1)}, u32[]{:S(2)}, u32[]{:S(2)}) %all-to-all-start) | async-done | bytes 3145760 | tf_op jit(solution)/shard_map/all_to_all | solution.py:165
  143.5 5.6 fusion.93
  149.1 6.2 fusion.82
  156.8 6.3 copy.80
  163.2 4.8 all-to-all-start.1
  169.0 136.6 %all-to-all-done.1 = f32[3,2,8,32,1024]{4,3,0,1,2:T(8,128)} async-done(((f32[3,2,8,32,1024]{4,3,0,1,2:T(8,128)}), f32[3,2,8,32,1024]{4,3,0,1,2:T(8,128)}, u32[]{:S(2)}, u32[]{:S(2)}) %all-to-all-start.1) | async-done | bytes 6291488 | tf_op jit(solution)/shard_map/all_to_all | solution.py:60
  310.1 48.0 %conditional.2 = ((f32[3,2,256,1024]{2,3,0,1:T(8,128)}, f32[3,2,256,1024]{2,3,0,1:T(8,128)})) conditional(s32[]{:T(128)} %convert_element_type.132, (f32[3,256,1024]{2,1,0:T(8,128)S(1)}, f32[256,256]{1,0:T(8,128)S(1)}, f32[3,256,1024]{2,1,0:T(8,128)S(1)}, f32[256,256]{1,0:T(8,128)S(1)}, f32[256,256]{1,0:T(8,128)S(1)}, ...), branch_computations={%region_0.1_spmd.clone, %region_1.2_spmd.clone} | conditional | flops 19338362880 | bytes 130027672 | solution.py:89
  335.7 5.6 fusion.74
  346.7 5.8 subtract_bitcast_fusion.5
  352.5 5.4 pad_maximum_fusion
  358.1 7.8 %multiply_subtract_fusion = (f32[1,2,256,1024]{2,3,0,1:T(8,128)}, f32[1,2,256,1024]{2,3,0,1:T(8,128)}) fusion(f32[3,2,256,1024]{2,3,0,1:T(8,128)} %get-tuple-element.306, f32[3,2,256,1024]{2,3,0,1:T(8,128)} %get-tuple-element.307), kind=kLoop, calls=%fused_computation.125 | loop fusion | flops 3145728 | bytes 16777216 | tf_op jit(solution)/shard_map/sub | solution.py:175
  377.6 41.3 %conditional.3 = (f32[3,1,256,1024]{3,2,0,1:T(8,128)}, f32[3,1,256,1024]{3,2,0,1:T(8,128)}) conditional(s32[]{:T(128)} %convert_element_type.132, (f32[3,2,256,1024]{2,3,0,1:T(8,128)S(1)}, f32[256,256]{1,0:T(8,128)S(1)}, f32[3,2,256,1024]{2,3,0,1:T(8,128)S(1)}, f32[256,256]{1,0:T(8,128)S(1)}, f32[256,256]{1,0:T(8,128)S(1)}, ...), branch_computations={%region_2.3_spmd, %region_3.4_spmd} | conditional | flops 14500233216 | bytes 165152912 | solution.py:110
  394.7 4.5 subtract_bitcast_fusion.2
  402.8 4.8 fusion.22
  423.0 139.4 %all_to_all.38 = f32[8,3,2,1,32,1024]{5,4,1,2,3,0:T(8,128)S(1)} all-to-all(f32[8,3,2,1,32,1024]{5,4,1,2,3,0:T(8,128)S(1)} %fusion.106), channel_id=1, replica_groups=mesh['ctx'=8,'ch'=4] {'ctx'}, dimensions={0} | all-to-all | bytes 12582912 | tf_op jit(solution)/shard_map/all_to_all | solution.py:113
  570.3 4.6 multiply_bitcast_fusion
  577.0 73.8 %all_to_all.39 = f32[3,8,32,1024]{3,2,0,1:T(8,128)S(1)} all-to-all(f32[3,8,32,1024]{3,2,0,1:T(8,128)S(1)} %copy.89), channel_id=1, replica_groups=mesh['ctx'=8,'ch'=4] {'ctx'}, dimensions={1} | all-to-all | bytes 6291456 | tf_op jit(solution)/shard_map/all_to_all | solution.py:184
  655.8 4.4 collective-permute-done.1
  662.9 35.7 %all-reduce.2 = (f32[3,3,1024]{2,0,1:T(4,128)S(1)}, f32[1024]{0:T(1024)}) all-reduce(f32[3,3,1024]{2,0,1:T(4,128)S(1)} %pad_maximum_fusion.7, f32[1024]{0:T(1024)S(1)} %get-tuple-element.330), channel_id=1, replica_groups=mesh['ctx'=8,'ch'=4] {'ctx'}, use_global_device_ids=true, to_apply=%region_7.8 | all-reduce | flops 10240 | bytes 81920 | tf_op jit(solution)/shard_map/psum | solution.py:206
  (126 shorter events, 92.3 us)
Async XLA Ops:
  7.2 7.8 %copy-start.23 = (bf16[256,1024]{1,0:T(8,128)(2,1)S(1)}, bf16[256,1024]{1,0:T(8,128)(2,1)}, u32[]{:S(2)}) copy-start(bf16[256,1024]{1,0:T(8,128)(2,1)} %param.14) | copy-start | bytes 1572868
  7.2 7.8 %copy-start.24 = (bf16[256,1024]{1,0:T(8,128)(2,1)S(1)}, bf16[256,1024]{1,0:T(8,128)(2,1)}, u32[]{:S(2)}) copy-start(bf16[256,1024]{1,0:T(8,128)(2,1)} %param.13) | copy-start | bytes 1572868
  7.2 7.8 %copy-start.25 = (bf16[256,1024]{1,0:T(8,128)(2,1)S(1)}, bf16[256,1024]{1,0:T(8,128)(2,1)}, u32[]{:S(2)}) copy-start(bf16[256,1024]{1,0:T(8,128)(2,1)} %param.12) | copy-start | bytes 1572868
  7.2 39.6 %all-gather.2.cloned.1.call-start = ((), (), s32[]{:S(2)}) async-start(), calls=%async_computation.4 | async-start | bytes 5242880 | tf_op jit(solution)/shard_map/all_gather | solution.py:157
  8.7 6.3 collective-permute-start
  17.1 42.0 %copy-start.15 = (f32[3,256,1024]{2,1,0:T(8,128)}, f32[3,256,1024]{2,1,0:T(8,128)S(1)}, u32[]{:S(2)}) copy-start(f32[3,256,1024]{2,1,0:T(8,128)S(1)} %multiply_add_fusion) | copy-start | bytes 9437188
  66.1 76.6 %all-to-all-start = ((f32[3,1,256,1024]{3,1,0,2:T(1,128)}), f32[3,1,256,1024]{3,1,0,2:T(1,128)S(1)}, u32[]{:S(2)}, u32[]{:S(2)}) async-start(f32[3,1,256,1024]{3,1,0,2:T(1,128)} %copy.76), calls=%async_computation | async-start | bytes 6291456 | tf_op jit(solution)/shard_map/all_to_all | solution.py:165
  163.2 142.5 %all-to-all-start.1 = ((f32[3,2,8,32,1024]{4,3,0,1,2:T(8,128)}), f32[3,2,8,32,1024]{4,3,0,1,2:T(8,128)}, u32[]{:S(2)}, u32[]{:S(2)}) async-start(f32[3,2,8,32,1024]{4,3,0,1,2:T(8,128)} %copy.80), calls=%async_computation.1 | async-start | bytes 12582912 | tf_op jit(solution)/shard_map/all_to_all | solution.py:60
  169.0 141.1 %copy-start.11 = (f32[256,256]{1,0:T(8,128)}, f32[256,256]{1,0:T(8,128)S(1)}, u32[]{:S(2)}) copy-start(f32[256,256]{1,0:T(8,128)S(1)} %get-tuple-element.345) | copy-start | bytes 786436
  332.8 2.9 copy-start.3
  358.1 7.9 %copy-start.8 = (f32[3,2,256,1024]{2,3,0,1:T(8,128)S(1)}, f32[3,2,256,1024]{2,3,0,1:T(8,128)}, u32[]{:S(2)}) copy-start(f32[3,2,256,1024]{2,3,0,1:T(8,128)} %get-tuple-element.307) | copy-start | bytes 18874372
  358.1 9.8 %copy-start.9 = (f32[3,2,256,1024]{2,3,0,1:T(8,128)S(1)}, f32[3,2,256,1024]{2,3,0,1:T(8,128)}, u32[]{:S(2)}) copy-start(f32[3,2,256,1024]{2,3,0,1:T(8,128)} %get-tuple-element.306) | copy-start | bytes 18874372
  371.9 3.8 copy-start.18
  371.9 4.1 copy-start.19
  371.9 4.7 copy-start.20
  390.1 2.9 copy-start.4
  390.1 4.5 copy-start.6
  402.8 4.8 copy-start.5
  407.6 2.8 copy-start.7
  654.2 6.5 copy-start.1
  654.3 6.5 copy-start.28
  654.3 6.5 copy-start.30
  654.3 6.5 copy-start.32
  654.3 6.0 collective-permute-start.1
  (14 other events, 28.1 us)
Sparse Core Ops, SparseCore 0:
  9.6 37.1 all-gather.1
